TPU v7x, 32 devices: a whole 2x2x4 slice. The times are simulated.
32 devices in a mesh: group: 2 (over y), dom: 4 (over z), row: 4 (over x, core).
Axes of the slice: x: 2, y: 2, z: 4, core: 2. Of those that a mesh axis runs over, the one named last changes fastest.
Arguments:
- state: bfloat16 [8, 16, 10752], P(('group', 'dom'), 'row'), parts along dimension 0, may hold values from -6 to 6
- prev_pred: bfloat16 [8, 16, 10752], P(('group', 'dom'), 'row'), parts along dimension 0, may hold values from -6 to 6
- ancestors: int32 [8], P('group'), parts along dimension 0, may hold values from 0 to 3, as said below
- timestep: int32 [2], P('group'), parts along dimension 0, may hold values from 50 to 949
- w_in: bfloat16 [168, 256], replicated, may hold values from -0.5 to 0.5
- w_time: bfloat16 [256, 256], replicated, may hold values from -0.375 to 0.375
- w_qkv: bfloat16 [2, 256, 768], replicated, may hold values from -0.375 to 0.375
- w_attn_out: bfloat16 [2, 256, 256], replicated, may hold values from -0.375 to 0.375
- w_up: bfloat16 [2, 256, 1024], replicated, may hold values from -0.375 to 0.375
- w_down: bfloat16 [2, 1024, 256], replicated, may hold values from -0.1875 to 0.1875
- w_out: bfloat16 [256, 84], replicated, may hold values from -0.375 to 0.375
Outputs:
- new_state: bfloat16 [8, 16, 10752], P(('group', 'dom'), 'row'), parts along dimension 0
- new_pred: bfloat16 [8, 16, 10752], P(('group', 'dom'), 'row'), parts along dimension 0
There are 2 independent parts, one for each index of `group`. A program takes and returns all parts, laid end to end along the dimension named above; an argument that names none is the same for every part. Nothing has to cross between parts.
Inputs may be any that keep to these rules, and one draw needn't show every extreme that they name: ancestors[j] is the particle of the same group whose state particle j takes; the list never falls.
All inputs are finite; a program needn't handle non-finite values.
Results may differ from a plain program's by a relative error of at most 0.018.
Values may be sent and summed in bfloat16 or wider, within the bound.
A program may use at most 64 MiB of HBM per device.

v0:
```python
import math

import jax
import jax.numpy as jnp
from jax import lax
from jax.sharding import PartitionSpec as P

D = 256
HEADS = 8
CH = 84
COLS = 128
STEPS = 1000
STRIDE = 20


def rms_round(values_in):
    widened = values_in.astype(jnp.float32)
    scaled = widened * lax.rsqrt(jnp.mean(widened * widened, axis=-1, keepdims=True) + 1e-06)
    return scaled.astype(jnp.bfloat16)


def unit_rows(values_in):
    return values_in * lax.rsqrt(jnp.mean(values_in * values_in, axis=-1, keepdims=True) + 1e-06)


def rotate(values_in, span_len):
    half_size = values_in.shape[-1] // 2
    places = jnp.arange(span_len, dtype=jnp.float32)
    rates = jnp.exp(-math.log(10000.0) * jnp.arange(half_size, dtype=jnp.float32) / half_size)
    angles = places[:, None] * rates[None, :]
    cos_part = jnp.cos(angles)[:, None, None, :]
    sin_part = jnp.sin(angles)[:, None, None, :]
    leading = values_in[..., :half_size]
    trailing = values_in[..., half_size:]
    return jnp.concatenate(
        [leading * cos_part - trailing * sin_part, leading * sin_part + trailing * cos_part],
        axis=-1,
    )


def attend(normed, weight_qkv, weight_out):
    batch_size, span_len, side_len, model_width = normed.shape
    head_size = model_width // HEADS
    joined = jnp.dot(normed, weight_qkv, preferred_element_type=jnp.float32)
    queries = unit_rows(joined[..., :model_width]).reshape(
        batch_size, span_len, side_len, HEADS, head_size
    )
    key_rows = unit_rows(joined[..., model_width : 2 * model_width]).reshape(
        batch_size, span_len, side_len, HEADS, head_size
    )
    values = (
        joined[..., 2 * model_width :]
        .astype(jnp.bfloat16)
        .reshape(batch_size, span_len, side_len, HEADS, head_size)
    )
    queries = rotate(queries, span_len).astype(jnp.bfloat16)
    key_rows = rotate(key_rows, span_len).astype(jnp.bfloat16)
    scores = jnp.einsum(
        "blmhe,bkmhe->bmhlk", queries, key_rows, preferred_element_type=jnp.float32
    ) / math.sqrt(head_size)
    weights = jnp.exp(scores)
    shares = (weights / jnp.sum(weights, axis=-1, keepdims=True)).astype(jnp.bfloat16)
    mixture = jnp.einsum("bmhlk,bkmhe->blmhe", shares, values, preferred_element_type=jnp.float32)
    mixture = mixture.astype(jnp.bfloat16).reshape(batch_size, span_len, side_len, model_width)
    return jnp.dot(mixture, weight_out, preferred_element_type=jnp.float32)


def mix_tokens(hidden, weight_qkv, weight_out):
    return (hidden.astype(jnp.float32) + attend(rms_round(hidden), weight_qkv, weight_out)).astype(
        jnp.bfloat16
    )


def feed_forward(hidden, weight_up, weight_down):
    lifted = jnp.dot(rms_round(hidden), weight_up, preferred_element_type=jnp.float32)
    gated = jax.nn.gelu(lifted, approximate=True).astype(jnp.bfloat16)
    return (
        hidden.astype(jnp.float32) + jnp.dot(gated, weight_down, preferred_element_type=jnp.float32)
    ).astype(jnp.bfloat16)


def level(moment):
    cosine = jnp.cos((moment / STEPS + 0.008) / 1.008 * math.pi / 2.0)
    return cosine * cosine


def time_vector(timestep, w_time):
    moment = timestep[0].astype(jnp.float32)
    half_size = w_time.shape[0] // 2
    rates = jnp.exp(-math.log(10000.0) * jnp.arange(half_size, dtype=jnp.float32) / half_size)
    embedded = jnp.concatenate([jnp.sin(moment * rates), jnp.cos(moment * rates)])
    return jnp.dot(embedded, w_time.astype(jnp.float32), precision=lax.Precision.HIGHEST)


def network(state_rows, prev_rows, offset_vec, w_in, w_qkv, w_attn_out, w_up, w_down, w_out):
    part_count, row_count, flat_width = state_rows.shape
    joined = jnp.concatenate(
        [
            state_rows.reshape(part_count, row_count, COLS, CH),
            prev_rows.reshape(part_count, row_count, COLS, CH),
        ],
        axis=-1,
    )
    hidden = (jnp.dot(joined, w_in, preferred_element_type=jnp.float32) + offset_vec).astype(
        jnp.bfloat16
    )
    hidden = hidden.reshape(part_count * row_count, COLS, 1, D)
    hidden = mix_tokens(hidden, w_qkv[0], w_attn_out[0])
    hidden = feed_forward(hidden, w_up[0], w_down[0])
    hidden = hidden.reshape(part_count, row_count, COLS, D)
    columns = lax.all_to_all(hidden, "row", split_axis=2, concat_axis=1, tiled=True)
    columns = mix_tokens(columns, w_qkv[1], w_attn_out[1])
    hidden = lax.all_to_all(columns, "row", split_axis=1, concat_axis=2, tiled=True)
    hidden = feed_forward(hidden, w_up[1], w_down[1])
    predicted = jnp.dot(rms_round(hidden), w_out, preferred_element_type=jnp.float32).astype(
        jnp.bfloat16
    )
    predicted = predicted.reshape(part_count, row_count, flat_width)
    return predicted


def per_device(
    state, prev_pred, ancestors, timestep, w_in, w_time, w_qkv, w_attn_out, w_up, w_down, w_out
):
    offset_vec = time_vector(timestep, w_time)
    moment = timestep[0].astype(jnp.float32)
    level_now = level(moment)
    level_next = level(moment - STRIDE)
    chosen_state = lax.all_to_all(
        jnp.take(
            lax.all_to_all(state, "dom", split_axis=2, concat_axis=0, tiled=True), ancestors, axis=0
        ),
        "dom",
        split_axis=0,
        concat_axis=2,
        tiled=True,
    )
    own_pred = network(state, prev_pred, offset_vec, w_in, w_qkv, w_attn_out, w_up, w_down, w_out)
    predicted = lax.all_to_all(
        jnp.take(
            lax.all_to_all(own_pred, "dom", split_axis=2, concat_axis=0, tiled=True),
            ancestors,
            axis=0,
        ),
        "dom",
        split_axis=0,
        concat_axis=2,
        tiled=True,
    )
    widened = chosen_state.astype(jnp.float32)
    pred_wide = predicted.astype(jnp.float32)
    noise_est = (widened - jnp.sqrt(level_now) * pred_wide) / jnp.sqrt(1.0 - level_now)
    updated = (jnp.sqrt(level_next) * pred_wide + jnp.sqrt(1.0 - level_next) * noise_est).astype(
        jnp.bfloat16
    )
    return (updated, predicted)


def solution(mesh):
    in_specs = (
        P(("group", "dom"), "row", None),
        P(("group", "dom"), "row", None),
        P("group"),
        P("group"),
        P(),
        P(),
        P(),
        P(),
        P(),
        P(),
        P(),
    )
    out_specs = (P(("group", "dom"), "row", None), P(("group", "dom"), "row", None))
    return jax.shard_map(
        per_device, mesh=mesh, in_specs=in_specs, out_specs=out_specs, check_vma=False
    )
```

profile of v0, /device:TPU:0, one launch (start us, length us, event | category | flops | bytes accessed | tf_op | source)
XLA Modules:
  0.0 268.8 jit_solution(5302937269611741926)
XLA Ops:
  9.7 2.1 fusion.32
  12.7 4.4 %all-to-all-start = ((bf16[1,4,128,256]{3,1,0,2:T(4,128)(2,1)}), bf16[1,4,128,256]{3,1,0,2:T(4,128)(2,1)S(1)}, u32[]{:S(2)}, u32[]{:S(2)}) async-start(bf16[1,4,128,256]{3,1,0,2:T(4,128)(2,1)} %copy.77), calls=%async_computation | async-start | bytes 524288 | tf_op jit(solution)/shard_map/all_to_all | solution.py:111
  17.2 8.8 %copy.92 = bf16[1,4,10752]{1,0,2:T(2,128)(2,1)} copy(bf16[1,4,10752]{2,1,0:T(4,128)(2,1)S(1)} %copy-done.5) | data formatting | bytes 172032 | tf_op args[0]
  26.4 58.9 %reduce.19 = bf16[10752,4]{1,0:T(8,128)(2,1)S(1)} reduce(bf16[10752,1,4]{2,1,0:T(2,128)(2,1)} %bitcast.158, bf16[]{:T(256)} %broadcast.323), dimensions={1}, to_apply=%bitcast.139.reduce_sub_computation | reduce | bytes 172034
  85.3 5.9 %reshape.588 = bf16[4,2,5376]{2,1,0:T(2,128)(2,1)} reshape(bf16[10752,4]{1,0:T(8,128)(2,1)S(1)} %reduce.19) | data formatting | bytes 172032
  95.5 1.8 reshape.541
  97.3 1.8 reshape.540
  99.1 2.9 %fusion.121 = (f32[1,16,32,8,16]{4,3,2,1,0:T(8,128)S(1)}, f32[1,16,32,8,16]{4,3,2,1,0:T(8,128)S(1)}) fusion(f32[1,16,32,8,32]{4,3,2,1,0:T(8,128)} %reshape.540), kind=kLoop, calls=%fused_computation.183 | loop fusion | bytes 1048576 | tf_op jit(solution)/shard_map/slice | solution.py:33
  102.8 4.9 %fusion.35 = (bf16[16,32,8,16]{3,0,2,1:T(8,128)(2,1)S(1)}, bf16[16,32,8,16]{3,0,2,1:T(8,128)(2,1)S(1)}, bf16[16,32,8,16]{3,0,2,1:T(8,128)(2,1)S(1)}, bf16[16,32,8,16]{3,0,2,1:T(8,128)(2,1)S(1)}) fusion(f32[1,16,32,8,16]{4,3,2,1,0:T(8,128)S(1)} %get-tuple-element.12, f32[1,16,32,8,16]{4,3,2,1,0:T(8,128)S(1)} %get-tuple-element.11, ...), kind=kLoop, calls=%fused_computation.55 | loop fusion | flops 1048576 | bytes 1574912 | tf_op jit(solution)/shard_map/concatenate | solution.py:35
  112.3 3.4 %all-to-all-start.1 = ((bf16[1,16,32,256]{3,2,0,1:T(8,128)(2,1)}), bf16[1,16,32,256]{3,2,0,1:T(8,128)(2,1)S(1)}, u32[]{:S(2)}, u32[]{:S(2)}) async-start(bf16[1,16,32,256]{3,2,0,1:T(8,128)(2,1)} %fusion.31), calls=%async_computation.1 | async-start | bytes 524288 | tf_op jit(solution)/shard_map/all_to_all | solution.py:113
  115.8 6.0 %all-to-all-done.1 = bf16[1,16,32,256]{3,2,0,1:T(8,128)(2,1)S(1)} async-done(((bf16[1,16,32,256]{3,2,0,1:T(8,128)(2,1)}), bf16[1,16,32,256]{3,2,0,1:T(8,128)(2,1)S(1)}, u32[]{:S(2)}, u32[]{:S(2)}) %all-to-all-start.1) | async-done | bytes 262176 | tf_op jit(solution)/shard_map/all_to_all | solution.py:113
  121.7 5.7 %all-to-all-start.4 = ((bf16[4,2,5376]{2,1,0:T(2,128)(2,1)}), bf16[4,2,5376]{2,1,0:T(2,128)(2,1)S(1)}, u32[]{:S(2)}, u32[]{:S(2)}) async-start(bf16[4,2,5376]{2,1,0:T(2,128)(2,1)} %reshape.588), calls=%async_computation.4 | async-start | bytes 172032 | tf_op jit(solution)/shard_map/all_to_all | solution.py:131
  127.9 2.3 multiply_reduce_fusion
  130.8 8.8 %copy.89 = bf16[1,4,10752]{1,0,2:T(2,128)(2,1)} copy(bf16[1,4,10752]{2,1,0:T(4,128)(2,1)S(1)} %reshape.543) | data formatting | bytes 172032 | tf_op jit(solution)/shard_map/reshape | solution.py:118
  139.6 58.9 %reduce.20 = bf16[10752,4]{1,0:T(8,128)(2,1)S(1)} reduce(bf16[10752,1,4]{2,1,0:T(2,128)(2,1)} %bitcast.159, bf16[]{:T(256)} %broadcast.323), dimensions={1}, to_apply=%bitcast.137.reduce_sub_computation | reduce | bytes 172034
  198.5 5.9 %reshape.586 = bf16[4,2,5376]{2,1,0:T(2,128)(2,1)} reshape(bf16[10752,4]{1,0:T(8,128)(2,1)S(1)} %reduce.20) | data formatting | bytes 172032
  204.3 5.4 %all-to-all-start.2 = ((bf16[4,2,5376]{2,1,0:T(2,128)(2,1)}), bf16[4,2,5376]{2,1,0:T(2,128)(2,1)S(1)}, u32[]{:S(2)}, u32[]{:S(2)}) async-start(bf16[4,2,5376]{2,1,0:T(2,128)(2,1)} %reshape.586), calls=%async_computation.2 | async-start | bytes 172032 | tf_op jit(solution)/shard_map/all_to_all | solution.py:141
  209.8 7.2 %reshape.589 = bf16[10752,1,4]{2,1,0:T(2,128)(2,1)} reshape(bf16[4,2,5376]{2,1,0:T(2,128)(2,1)S(1)} %all-to-all-done.4) | data formatting | bytes 172032
  217.0 10.4 %copy.93 = bf16[1,4,10752]{2,1,0:T(4,128)(2,1)S(1)} copy(bf16[1,4,10752]{1,0,2:T(2,128)(2,1)} %bitcast.160) | data formatting | bytes 172032 | tf_op jit(solution)/shard_map/all_to_all | solution.py:131
  228.1 7.2 %reshape.587 = bf16[10752,1,4]{2,1,0:T(2,128)(2,1)} reshape(bf16[4,2,5376]{2,1,0:T(2,128)(2,1)S(1)} %all-to-all-done.2) | data formatting | bytes 172032
  235.3 10.5 %copy.90 = bf16[1,4,10752]{2,1,0:T(4,128)(2,1)S(1)} copy(bf16[1,4,10752]{1,0,2:T(2,128)(2,1)} %bitcast.161) | data formatting | bytes 172032 | tf_op jit(solution)/shard_map/all_to_all | solution.py:141
  247.2 10.7 %all_to_all.81 = bf16[4,4,2688]{2,1,0:T(4,128)(2,1)S(1)} all-to-all(bf16[4,4,2688]{2,1,0:T(4,128)(2,1)S(1)} %get-tuple-element.28), channel_id=1, replica_groups=mesh['group'=2,'dom'=4,'row'=4] {'dom'}, dimensions={0} | all-to-all | bytes 172032 | tf_op jit(solution)/shard_map/all_to_all | solution.py:139
  257.8 3.3 %all-to-all-start.5 = ((bf16[4,4,2688]{2,1,0:T(4,128)(2,1)}), bf16[4,4,2688]{2,1,0:T(4,128)(2,1)S(1)}, u32[]{:S(2)}, u32[]{:S(2)}) async-start(bf16[4,4,2688]{2,1,0:T(4,128)(2,1)} %get-tuple-element.27), calls=%async_computation.5 | async-start | bytes 172032 | tf_op jit(solution)/shard_map/all_to_all | solution.py:129
  261.5 5.4 %all-to-all-done.5 = bf16[4,4,2688]{2,1,0:T(4,128)(2,1)S(1)} async-done(((bf16[4,4,2688]{2,1,0:T(4,128)(2,1)}), bf16[4,4,2688]{2,1,0:T(4,128)(2,1)S(1)}, u32[]{:S(2)}, u32[]{:S(2)}) %all-to-all-start.5) | async-done | bytes 86048 | tf_op jit(solution)/shard_map/all_to_all | solution.py:129
  (86 shorter events, 23.6 us)
Async XLA Ops:
  0.6 3.8 %copy-start = (bf16[256,256]{1,0:T(8,128)(2,1)S(1)}, bf16[256,256]{1,0:T(8,128)(2,1)}, u32[]{:S(2)}) copy-start(bf16[256,256]{1,0:T(8,128)(2,1)} %param.18) | copy-start | bytes 393220
  0.6 5.3 %copy-start.3 = (bf16[2,256,768]{2,1,0:T(8,128)(2,1)S(1)}, bf16[2,256,768]{2,1,0:T(8,128)(2,1)}, u32[]{:S(2)}) copy-start(bf16[2,256,768]{2,1,0:T(8,128)(2,1)} %param.19) | copy-start | bytes 2359300
  8.3 1.0 copy-start.6
  8.3 1.3 copy-start.8
  9.7 7.5 %copy-start.5 = (bf16[1,4,10752]{2,1,0:T(4,128)(2,1)S(1)}, bf16[1,4,10752]{2,1,0:T(4,128)(2,1)}, u32[]{:S(2)}) copy-start(bf16[1,4,10752]{2,1,0:T(4,128)(2,1)} %param.13) | copy-start | bytes 258052
  12.7 78.5 %all-to-all-start = ((bf16[1,4,128,256]{3,1,0,2:T(4,128)(2,1)}), bf16[1,4,128,256]{3,1,0,2:T(4,128)(2,1)S(1)}, u32[]{:S(2)}, u32[]{:S(2)}) async-start(bf16[1,4,128,256]{3,1,0,2:T(4,128)(2,1)} %copy.77), calls=%async_computation | async-start | bytes 524288 | tf_op jit(solution)/shard_map/all_to_all | solution.py:111
  91.3 1.1 copy-start.4
  107.7 1.7 copy-start.2
  110.4 5.3 %copy-start.9 = (s32[4]{0:T(128)S(1)}, s32[4]{0:T(128)}, u32[]{:S(2)}) copy-start(s32[4]{0:T(128)} %param.15) | copy-start | bytes 52
  112.3 9.4 %all-to-all-start.1 = ((bf16[1,16,32,256]{3,2,0,1:T(8,128)(2,1)}), bf16[1,16,32,256]{3,2,0,1:T(8,128)(2,1)S(1)}, u32[]{:S(2)}, u32[]{:S(2)}) async-start(bf16[1,16,32,256]{3,2,0,1:T(8,128)(2,1)} %fusion.31), calls=%async_computation.1 | async-start | bytes 524288 | tf_op jit(solution)/shard_map/all_to_all | solution.py:113
  121.7 82.6 %all-to-all-start.4 = ((bf16[4,2,5376]{2,1,0:T(2,128)(2,1)}), bf16[4,2,5376]{2,1,0:T(2,128)(2,1)S(1)}, u32[]{:S(2)}, u32[]{:S(2)}) async-start(bf16[4,2,5376]{2,1,0:T(2,128)(2,1)} %reshape.588), calls=%async_computation.4 | async-start | bytes 172032 | tf_op jit(solution)/shard_map/all_to_all | solution.py:131
  127.9 2.3 copy-start.7
  204.3 23.7 %all-to-all-start.2 = ((bf16[4,2,5376]{2,1,0:T(2,128)(2,1)}), bf16[4,2,5376]{2,1,0:T(2,128)(2,1)S(1)}, u32[]{:S(2)}, u32[]{:S(2)}) async-start(bf16[4,2,5376]{2,1,0:T(2,128)(2,1)} %reshape.586), calls=%async_computation.2 | async-start | bytes 172032 | tf_op jit(solution)/shard_map/all_to_all | solution.py:141
  235.3 33.0 %copy-start.1 = (bf16[256,256]{1,0:T(8,128)(2,1)S(1)}, bf16[256,256]{1,0:T(8,128)(2,1)}, u32[]{:S(2)}) copy-start(bf16[256,256]{1,0:T(8,128)(2,1)} %param.18) | copy-start | bytes 393220
  257.8 9.1 %all-to-all-start.5 = ((bf16[4,4,2688]{2,1,0:T(4,128)(2,1)}), bf16[4,4,2688]{2,1,0:T(4,128)(2,1)S(1)}, u32[]{:S(2)}, u32[]{:S(2)}) async-start(bf16[4,4,2688]{2,1,0:T(4,128)(2,1)} %get-tuple-element.27), calls=%async_computation.5 | async-start | bytes 172032 | tf_op jit(solution)/shard_map/all_to_all | solution.py:129
where the time goes:
time: 274 us; the launch traced here: 269 us
  other arithmetic  127 us (46%)
  local copies, waits for them, and re-layouts  82.9 us (30%)
  starting transfers between devices  22.2 us (8%)
  matrix products  11.9 us (4%)
  waiting for transfers between devices  11.4 us (4%)
  blocking collectives  10.7 us (4%)
    unnamed x2, other arithmetic  118 us
    unnamed x27, local copies, waits for them, and re-layouts  37.3 us
    all_to_all x1, blocking collectives, per_device(): lax.all_to_all(jnp.take(lax.all_to_all(own_pred, 'dom', split_axis=2, con...  10.7 us
    all_to_all x1, local copies, waits for them, and re-layouts, per_device(): lax.all_to_all(own_pred, 'dom', split_axis=2, concat_axis=0, tiled=True)  10.5 us
    all_to_all x1, local copies, waits for them, and re-layouts, per_device(): lax.all_to_all(state, 'dom', split_axis=2, concat_axis=0, tiled=True)  10.4 us
    reshape x2, local copies, waits for them, and re-layouts, network(): predicted = predicted.reshape(part_count, row_count, flat_width)  9 us
    all_to_all x1, waiting for transfers between devices, network(): lax.all_to_all(columns, 'row', split_axis=1, concat_axis=2, tiled=True)  5.97 us
    all_to_all x1, starting transfers between devices, per_device(): lax.all_to_all(state, 'dom', split_axis=2, concat_axis=0, tiled=True)  5.74 us
  transfers between devices with their start and end apart: 5, of which 2 were waited for; matrix products, arithmetic and copies ran while one was open for 63% of the time, Pallas kernels for 0%

commit v1 on v0

v1 whole, which is shorter than its diff:
```python
import functools
import math

import jax
import jax.numpy as jnp
import numpy as np
from jax import lax
from jax.experimental import pallas as pl
from jax.experimental.pallas import tpu as pltpu
from jax.sharding import PartitionSpec as P

HEADS = 8
STEPS = 1000
STRIDE = 20
LANES = 128
MESH = pl.DeviceIdType.MESH
F32 = jnp.float32
BF16 = jnp.bfloat16


def rms(v):
    return v * lax.rsqrt(jnp.mean(v * v, axis=-1, keepdims=True) + 1e-06)


def mm(a, b):
    return jnp.dot(a, b, preferred_element_type=F32)


def mm_nt(a, b):
    return lax.dot_general(a, b, (((1,), (1,)), ((), ())), preferred_element_type=F32)


def rope_tables(length, head):
    half = head // 2
    rates = np.exp(-math.log(10000.0) * np.arange(half) / half)
    angles = np.arange(length)[:, None] * rates[None, :]
    reps = LANES // head
    cos = np.tile(np.concatenate([np.cos(angles), np.cos(angles)], axis=1), (1, reps))
    sin = np.tile(np.concatenate([-np.sin(angles), np.sin(angles)], axis=1), (1, reps))
    return cos.astype(np.float32), sin.astype(np.float32)


def rotated(v, cos, sin, head):
    inv = lax.rsqrt(jnp.mean(v * v, axis=-1, keepdims=True) + 1e-06)
    lane = lax.broadcasted_iota(jnp.int32, (1, LANES), 1)
    low = (lane % head) < head // 2
    parts = []
    for part in range(v.shape[1] // LANES):
        x = v[:, part * LANES : (part + 1) * LANES]
        partner = jnp.where(
            low,
            pltpu.roll(x, LANES - head // 2, 1),
            pltpu.roll(x, head // 2, 1),
        )
        parts.append((x * cos + partner * sin) * inv)
    return parts


def attention(q, k, v, mask, head):
    n = q[0].shape[0]
    lane = lax.broadcasted_iota(jnp.int32, (1, LANES), 1)
    per = LANES // head
    scale = math.log2(math.e) / math.sqrt(head)
    outs = []
    for part in range(len(q)):
        keys, vals = [], []
        for h in range(per):
            pick = jnp.where(lane // head == h, 1.0, 0.0).astype(BF16)
            keys.append(k[part] * pick)
            vals.append(
                jnp.concatenate([v[part] * pick, jnp.broadcast_to(pick, (n, LANES))], axis=1)
            )
        scores = mm_nt(q[part], jnp.concatenate(keys, axis=0))
        weights = jnp.exp2(scores * scale)
        if mask is not None:
            weights = weights * mask
        both = mm(weights.astype(BF16), jnp.concatenate(vals, axis=0))
        outs.append(both[:, :LANES] / both[:, LANES:])
    return jnp.concatenate(outs, axis=1).astype(BF16)


def mlp(h, w_up, w_down):
    lifted = mm(rms(h).astype(BF16), w_up)
    gated = jax.nn.gelu(lifted, approximate=True).astype(BF16)
    return (h + mm(gated, w_down)).astype(BF16)


def kernel(
    cfg,
    anc_ref, coef_ref, state_ref, prev_ref, emb_ref, tab_ref, w_in_ref, w_time_ref,
    w_qkv_hbm, w_attn_hbm, w_up_hbm, w_down_hbm, w_out_ref,
    new_state_ref, new_pred_ref,
    w_qkv, w_attn, w_up, w_down,
    xs, xp, h1, hcol, psend, ptok, states, preds,
    w_sem, own_sem, st_send, st_recv, h_send, h_recv, p_send, p_recv, g_send, g_recv,
):
    ndom, nrow, rows, cols, ch, d, head, height = cfg
    dom, row = lax.axis_index("dom"), lax.axis_index("row")
    mine = cols // nrow
    width = cols * ch
    group = LANES // math.gcd(ch, LANES)
    glanes = group * ch

    loads = []
    pairs = ((w_qkv_hbm, w_qkv), (w_attn_hbm, w_attn), (w_up_hbm, w_up), (w_down_hbm, w_down))
    for b in range(2):
        for i, (src, dst) in enumerate(pairs):
            copy = pltpu.make_async_copy(src.at[b], dst.at[b], w_sem.at[b, i])
            copy.start()
            loads.append(copy)

    barrier = pltpu.get_barrier_semaphore()
    for k in range(1, ndom):
        pl.semaphore_signal(
            barrier, inc=1, device_id={"dom": lax.rem(dom + k, ndom)}, device_id_type=MESH
        )
    for k in range(1, nrow):
        pl.semaphore_signal(
            barrier, inc=1, device_id={"row": lax.rem(row + k, nrow)}, device_id_type=MESH
        )
    own = pltpu.make_async_copy(state_ref.at[0], states.at[dom], own_sem)
    own.start()

    lane = lax.broadcasted_iota(jnp.int32, (rows, LANES), 1)

    def split(c, carry):
        base = pl.multiple_of(c * glanes, LANES)
        for ref, out in ((state_ref, xs), (prev_ref, xp)):
            tiles = [
                ref[0, :, pl.ds(pl.multiple_of(base + j * LANES, LANES), LANES)].astype(F32)
                for j in range(glanes // LANES)
            ]
            for t in range(group):
                j, off = divmod(t * ch, LANES)
                v = pltpu.roll(tiles[j], LANES - off, 1) if off else tiles[j]
                if off + ch > LANES:
                    v = jnp.where(lane < LANES - off, v, pltpu.roll(tiles[j + 1], LANES - off, 1))
                out[pl.ds(c * group + t, rows, stride=cols), :] = v
        return carry

    lax.fori_loop(0, cols // group, split, 0)

    pl.semaphore_wait(barrier, ndom - 1 + nrow - 1)
    sends = []
    for k in range(1, ndom):
        copy = pltpu.make_async_remote_copy(
            src_ref=state_ref.at[0],
            dst_ref=states.at[dom],
            send_sem=st_send.at[k],
            recv_sem=st_recv.at[k],
            device_id={"dom": lax.rem(dom + k, ndom)},
            device_id_type=MESH,
        )
        copy.start()
        sends.append(copy)

    temb = jnp.dot(
        emb_ref[...], w_time_ref[...].astype(F32),
        precision=lax.Precision.HIGHEST, preferred_element_type=F32,
    )[0:1]
    w_in = w_in_ref[...].astype(F32)
    w_in_s, w_in_p = w_in[:ch].astype(BF16), w_in[ch:].astype(BF16)

    for copy in loads[:4]:
        copy.wait()
    cos_r, sin_r = tab_ref[0:cols], tab_ref[cols : 2 * cols]
    step_rows = 2 if rows % 2 == 0 else 1
    n0 = step_rows * cols

    def first(i, carry):
        sl = pl.ds(pl.multiple_of(i * n0, n0), n0)
        h = mm(xs[sl, :ch].astype(BF16), w_in_s) + mm(xp[sl, :ch].astype(BF16), w_in_p) + temb
        h = h.astype(BF16).astype(F32)
        qkv = mm(rms(h).astype(BF16), w_qkv[0])
        cos = jnp.concatenate([cos_r] * step_rows, axis=0)
        sin = jnp.concatenate([sin_r] * step_rows, axis=0)
        q = [x.astype(BF16) for x in rotated(qkv[:, :d], cos, sin, head)]
        k = [x.astype(BF16) for x in rotated(qkv[:, d : 2 * d], cos, sin, head)]
        v = qkv[:, 2 * d :].astype(BF16)
        v = [v[:, p * LANES : (p + 1) * LANES] for p in range(d // LANES)]
        mixed = []
        for r in range(step_rows):
            a, b = r * cols, (r + 1) * cols
            mixed.append(
                attention([x[a:b] for x in q], [x[a:b] for x in k], [x[a:b] for x in v], None, head)
            )
        o = jnp.concatenate(mixed, axis=0)
        h = (h + mm(o, w_attn[0])).astype(BF16).astype(F32)
        h = mlp(h, w_up[0], w_down[0])
        h1[pl.ds(i * step_rows, step_rows)] = h.reshape(step_rows, cols, d)
        return carry

    lax.fori_loop(0, rows // step_rows, first, 0)

    hs = []
    for k in range(1, nrow):
        peer = lax.rem(row + k, nrow)
        copy = pltpu.make_async_remote_copy(
            src_ref=h1.at[:, pl.ds(pl.multiple_of(peer * mine, mine), mine), :],
            dst_ref=hcol.at[pl.ds(row * rows, rows)],
            send_sem=h_send.at[k],
            recv_sem=h_recv.at[k],
            device_id={"row": peer},
            device_id_type=MESH,
        )
        copy.start()
        hs.append(copy)
    hcol[pl.ds(row * rows, rows)] = h1[:, pl.ds(pl.multiple_of(row * mine, mine), mine), :]
    for copy in loads[4:]:
        copy.wait()
    for copy in hs:
        copy.wait_recv()

    cos_c = tab_ref[2 * cols : 2 * cols + 8 * height].reshape(height, 8, LANES)
    sin_c = tab_ref[2 * cols + 8 * height : 2 * cols + 16 * height].reshape(height, 8, LANES)
    wide = 16
    n1 = height * wide
    sub = height * 8
    cos_c = jnp.concatenate([cos_c, cos_c], axis=1).reshape(n1, LANES)
    sin_c = jnp.concatenate([sin_c, sin_c], axis=1).reshape(n1, LANES)
    per = LANES // head
    qi = lax.broadcasted_iota(jnp.int32, (sub, per * sub), 0)
    ki = lax.broadcasted_iota(jnp.int32, (sub, per * sub), 1)
    mask = jnp.where(qi % 8 == ki % 8, 1.0, 0.0).astype(F32)

    def second(i, carry):
        sl = pl.ds(pl.multiple_of(i * wide, wide), wide)
        h = hcol[:, sl, :].reshape(n1, d).astype(F32)
        qkv = mm(rms(h).astype(BF16), w_qkv[1])
        q = rotated(qkv[:, :d], cos_c, sin_c, head)
        k = rotated(qkv[:, d : 2 * d], cos_c, sin_c, head)
        v = [qkv[:, 2 * d + p * LANES : 2 * d + (p + 1) * LANES] for p in range(d // LANES)]
        mixed = []
        for s in range(wide // 8):

            def cut(xs_):
                return [
                    x.reshape(height, wide, LANES)[:, 8 * s : 8 * s + 8, :]
                    .reshape(sub, LANES)
                    .astype(BF16)
                    for x in xs_
                ]

            o = attention(cut(q), cut(k), cut(v), mask, head)
            mixed.append(o.astype(F32).reshape(height, 8, d))
        o = jnp.concatenate(mixed, axis=1).reshape(n1, d).astype(BF16)
        h = (h + mm(o, w_attn[1])).astype(BF16).astype(F32)
        h = mlp(h, w_up[1], w_down[1]).astype(F32)
        pred = mm(rms(h).astype(BF16), w_out_ref[...])
        psend[:, sl, 0:ch] = pred.astype(BF16).reshape(height, wide, ch)
        return carry

    lax.fori_loop(0, mine // wide, second, 0)

    ps = []
    for k in range(1, nrow):
        peer = lax.rem(row + k, nrow)
        copy = pltpu.make_async_remote_copy(
            src_ref=psend.at[pl.ds(peer * rows, rows)],
            dst_ref=ptok.at[:, pl.ds(pl.multiple_of(row * mine, mine), mine), :],
            send_sem=p_send.at[k],
            recv_sem=p_recv.at[k],
            device_id={"row": peer},
            device_id_type=MESH,
        )
        copy.start()
        ps.append(copy)
    ptok[:, pl.ds(pl.multiple_of(row * mine, mine), mine), :] = psend[pl.ds(row * rows, rows)]
    for copy in ps:
        copy.wait_recv()
    for r in range(rows):
        xs[r * cols : (r + 1) * cols, :] = ptok[r].astype(F32)

    def join(c, carry):
        base = c * glanes
        toks = [xs[pl.ds(c * group + t, rows, stride=cols), :] for t in range(group)]
        for j in range(glanes // LANES):
            first_t, last_t = (j * LANES) // ch, (j * LANES + LANES - 1) // ch
            acc = None
            for t in range(first_t, last_t + 1):
                s = t * ch - j * LANES
                v = pltpu.roll(toks[t], s % LANES, 1) if s % LANES else toks[t]
                acc = v if acc is None else jnp.where(lane >= s, v, acc)
            preds[dom, :, pl.ds(pl.multiple_of(base + j * LANES, LANES), LANES)] = acc.astype(BF16)
        return carry

    lax.fori_loop(0, cols // group, join, 0)

    gs = []
    for k in range(1, ndom):
        copy = pltpu.make_async_remote_copy(
            src_ref=preds.at[dom],
            dst_ref=preds.at[dom],
            send_sem=g_send.at[k],
            recv_sem=g_recv.at[k],
            device_id={"dom": lax.rem(dom + k, ndom)},
            device_id_type=MESH,
        )
        copy.start()
        gs.append(copy)
    own.wait()
    for copy in sends:
        copy.wait()
    for copy in gs:
        copy.wait()
    for copy in hs + ps:
        copy.wait_send()
    a = anc_ref[dom]
    c1, c2, c3 = coef_ref[0], coef_ref[1], coef_ref[2]
    for c in range(cols // group):
        sl = pl.ds(c * glanes, glanes)
        p = preds[a, :, sl]
        pw = p.astype(F32)
        st = states[a, :, sl].astype(F32)
        new_pred_ref[0, :, sl] = p
        new_state_ref[0, :, sl] = (c2 * pw + c3 * (st - c1 * pw)).astype(BF16)


def level(moment):
    cosine = jnp.cos((moment / STEPS + 0.008) / 1.008 * math.pi / 2.0)
    return cosine * cosine


def per_device(
    sizes, state, prev_pred, ancestors, timestep, w_in, w_time, w_qkv, w_attn_out, w_up, w_down, w_out
):
    ndom, nrow = sizes
    _, rows, width = state.shape
    d, ch = w_out.shape
    cols, height, head = width // ch, rows * nrow, d // HEADS
    ff = w_up.shape[2]
    moment = timestep[0].astype(F32)
    half = w_time.shape[0] // 2
    rates = jnp.exp(-math.log(10000.0) * jnp.arange(half, dtype=F32) / half)
    emb = jnp.concatenate([jnp.sin(moment * rates), jnp.cos(moment * rates)])
    emb = jnp.broadcast_to(emb[None], (8, 2 * half))
    now, nxt = level(moment), level(moment - STRIDE)
    coef = jnp.stack([jnp.sqrt(now), jnp.sqrt(nxt), jnp.sqrt(1.0 - nxt) / jnp.sqrt(1.0 - now)])
    cos_r, sin_r = rope_tables(cols, head)
    cos_c, sin_c = rope_tables(height, head)
    tables = jnp.asarray(
        np.concatenate([cos_r, sin_r, np.repeat(cos_c, 8, axis=0), np.repeat(sin_c, 8, axis=0)])
    )
    cfg = (ndom, nrow, rows, cols, ch, d, head, height)
    mine = cols // nrow
    smem = pl.BlockSpec(memory_space=pltpu.SMEM)
    vmem = pl.BlockSpec(memory_space=pltpu.VMEM)
    hbm = pl.BlockSpec(memory_space=pl.ANY)
    flat = jax.ShapeDtypeStruct((1, rows, width), BF16)
    dma = pltpu.SemaphoreType.DMA
    return pl.pallas_call(
        functools.partial(kernel, cfg),
        out_shape=(flat, flat),
        in_specs=[smem, smem, vmem, vmem, vmem, vmem, vmem, vmem, hbm, hbm, hbm, hbm, vmem],
        out_specs=(vmem, vmem),
        scratch_shapes=[
            pltpu.VMEM((2, d, 3 * d), BF16),
            pltpu.VMEM((2, d, d), BF16),
            pltpu.VMEM((2, d, ff), BF16),
            pltpu.VMEM((2, ff, d), BF16),
            pltpu.VMEM((rows * cols, LANES), F32),
            pltpu.VMEM((rows * cols, LANES), F32),
            pltpu.VMEM((rows, cols, d), BF16),
            pltpu.VMEM((height, mine, d), BF16),
            pltpu.VMEM((height, mine, LANES), BF16),
            pltpu.VMEM((rows, cols, LANES), BF16),
            pltpu.VMEM((ndom, rows, width), BF16),
            pltpu.VMEM((ndom, rows, width), BF16),
            dma((2, 4)),
            dma,
            dma((ndom,)),
            dma((ndom,)),
            dma((nrow,)),
            dma((nrow,)),
            dma((nrow,)),
            dma((nrow,)),
            dma((ndom,)),
            dma((ndom,)),
        ],
        compiler_params=pltpu.CompilerParams(
            collective_id=0, has_side_effects=True, vmem_limit_bytes=56 * 1024 * 1024
        ),
    )(
        ancestors, coef, state, prev_pred, emb, tables, w_in, w_time,
        w_qkv, w_attn_out, w_up, w_down, w_out,
    )


def solution(mesh):
    part = P(("group", "dom"), "row", None)
    in_specs = (part, part, P("group"), P("group")) + (P(),) * 7
    return jax.shard_map(
        functools.partial(per_device, (mesh.shape["dom"], mesh.shape["row"])),
        mesh=mesh, in_specs=in_specs, out_specs=(part, part), check_vma=False,
    )
```

time: 274 us -> 39.8 us (0.15); the launches traced: 269 us -> 39.6 us
  other arithmetic: 127 us -> 0.71 us
  local copies, waits for them, and re-layouts: 82.9 us -> 3.57 us
  Pallas kernels: 0 us -> 33.7 us
  starting transfers between devices: 22.2 us -> 0 us
  matrix products: 11.9 us -> 0 us
  waiting for transfers between devices: 11.4 us -> 0 us
  blocking collectives: 10.7 us -> 0 us
    unnamed x2 -> x0, other arithmetic: 118 us -> none
    unnamed x27 -> x7, local copies, waits for them, and re-layouts: 37.3 us -> 2.97 us
    pallas_call x0 -> x1, Pallas kernels: none -> 33.7 us  [per_device(): pl.pallas_call(functools.partial(kernel, cfg), out_shape=(flat, flat), in...]
    all_to_all x5 -> x0, starting transfers between devices: 22.2 us -> none  [the longest x1 5.74 us: per_device(): lax.all_to_all(state, 'dom', split_axis=2, concat_axis=0, tiled=True)]
    all_to_all x2 -> x0, local copies, waits for them, and re-layouts: 20.9 us -> none  [the longest x1 10.5 us: per_device(): lax.all_to_all(own_pred, 'dom', split_axis=2, concat_axis=0, tiled=True)]
    reshape x9 -> x0, local copies, waits for them, and re-layouts: 16.5 us -> none  [the longest x2 9 us: network(): predicted = predicted.reshape(part_count, row_count, flat_width)]
    dot_general x13 -> x0, matrix products: 11.9 us -> none  [the longest x2 4.33 us: feed_forward(): jnp.dot(gated, weight_down, preferred_element_type=jnp.float32)]
    all_to_all x5 -> x0, waiting for transfers between devices: 11.4 us -> none  [the longest x1 5.97 us: network(): lax.all_to_all(columns, 'row', split_axis=1, concat_axis=2, tiled=True)]
  transfers between devices with their start and end apart: 5 -> 0, of which waited for: 2 -> 0; matrix products, arithmetic and copies ran while one was open for 63% -> 0% of each run, Pallas kernels for 0% -> 0%
where the time goes in v1:
time: 39.8 us; the launch traced here: 39.6 us
  Pallas kernels  33.7 us (85%)
  local copies, waits for them, and re-layouts  3.57 us (9%)
  between operations  1.65 us (4%)
  other arithmetic  0.71 us (2%)
    pallas_call x1, Pallas kernels, per_device(): pl.pallas_call(functools.partial(kernel, cfg), out_shape=(flat, flat), in...  33.7 us
    unnamed x7, local copies, waits for them, and re-layouts  2.97 us

profile of v1, /device:TPU:0, one launch (start us, length us, event | category | flops | bytes accessed | tf_op | source)
XLA Modules:
  0.0 39.6 jit_solution(1885049206786172993)
XLA Ops:
  0.6 0.0 copy-start.1
  1.6 0.6 %pad_maximum_fusion.1.coef_ref = f32[3]{0:T(128)} fusion(f32[1]{0:T(128)} %bitcast.3, f32[1]{0:T(128)} %bitcast.2, f32[1]{0:T(128)} %bitcast.1), kind=kLoop, calls=%fused_computation.1 | loop fusion | flops 6 | bytes 24 | tf_op jit(solution)/shard_map/stack | solution.py:338
  2.3 0.6 %broadcast_in_dim.2.emb_ref = f32[8,256]{1,0:T(8,128)} broadcast(f32[256]{0:T(256)S(1)} %pad_maximum_fusion), dimensions={1} | broadcast | bytes 9216 | tf_op jit(solution)/shard_map/broadcast_in_dim | solution.py:336
  2.9 0.0 copy-done.1
  2.9 0.7 %copy.14.w_out_ref = bf16[256,84]{1,0:T(8,128)(2,1)} copy(bf16[256,84]{0,1:T(8,128)(2,1)S(1)} %copy-done.1) | data formatting | bytes 86016 | tf_op args[10]
  3.7 33.7 %shard_map.131 = (bf16[1,4,10752]{2,1,0:T(4,128)(2,1)}, bf16[1,4,10752]{2,1,0:T(4,128)(2,1)}) custom-call(s32[4]{0:T(128)} %anc_ref.1, f32[3]{0:T(128)} %pad_maximum_fusion.1.coef_ref, bf16[1,4,10752]{2,1,0:T(4,128)(2,1)} %state_ref.1, bf16[1,4,10752]{2,1,0:T(4,128)(2,1)} %prev_ref.1, f32[8,256]{1,0:T(8,128)} %broadcast_in_dim.2.emb_ref, ...), custom_call_target="tpu_custom_call" | custom-call | tf_op jit(solution)/shard_map/pallas_call | solution.py:351
  37.4 0.0 copy-start
  37.4 1.6 %copy.18 = bf16[1,4,10752]{2,1,0:T(4,128)(2,1)} copy(bf16[1,4,10752]{2,1,0:T(4,128)(2,1)} %get-tuple-element.6) | data formatting | bytes 172032
  39.0 0.0 copy-done
  39.0 0.6 %copy.19 = bf16[1,4,10752]{2,1,0:T(4,128)(2,1)} copy(bf16[1,4,10752]{2,1,0:T(4,128)(2,1)S(1)} %copy-done) | data formatting | bytes 172032
  (2 shorter events, 0.1 us)
Async XLA Ops:
  0.6 2.3 %copy-start.1 = (bf16[256,84]{0,1:T(8,128)(2,1)S(1)}, bf16[256,84]{0,1:T(8,128)(2,1)}, u32[]{:S(2)}) copy-start(bf16[256,84]{0,1:T(8,128)(2,1)} %param.22) | copy-start | bytes 129028
  37.4 1.6 %copy-start = (bf16[1,4,10752]{2,1,0:T(4,128)(2,1)S(1)}, bf16[1,4,10752]{2,1,0:T(4,128)(2,1)}, u32[]{:S(2)}) copy-start(bf16[1,4,10752]{2,1,0:T(4,128)(2,1)} %get-tuple-element.7) | copy-start | bytes 258052

commit v2 on v1

--- a/solution.py
+++ b/solution.py
@@ -87,19 +87,19 @@
 
 def kernel(
     cfg,
-    anc_ref, coef_ref, state_ref, prev_ref, emb_ref, tab_ref, w_in_ref, w_time_ref,
+    anc_ref, time_ref, state_ref, prev_ref, tab_ref, w_in_ref, w_time_ref,
     w_qkv_hbm, w_attn_hbm, w_up_hbm, w_down_hbm, w_out_ref,
-    new_state_ref, new_pred_ref,
+    state_out, pred_out,
     w_qkv, w_attn, w_up, w_down,
-    xs, xp, h1, hcol, psend, ptok, states, preds,
-    w_sem, own_sem, st_send, st_recv, h_send, h_recv, p_send, p_recv, g_send, g_recv,
+    xs, xp, h1, hcol, ptok, gat, selw, sel, fin, states,
+    w_sem, own_sem, st_send, st_recv, h_send, h_recv, g_send, g_recv, p_send, p_recv,
 ):
-    ndom, nrow, rows, cols, ch, d, head, height = cfg
+    ndom, nrow, rows, cols, ch, d, head, height, wide, flat = cfg
     dom, row = lax.axis_index("dom"), lax.axis_index("row")
     mine = cols // nrow
-    width = cols * ch
     group = LANES // math.gcd(ch, LANES)
     glanes = group * ch
+    halves = mine // wide
 
     loads = []
     pairs = ((w_qkv_hbm, w_qkv), (w_attn_hbm, w_attn), (w_up_hbm, w_up), (w_down_hbm, w_down))
@@ -140,6 +140,17 @@
 
     lax.fori_loop(0, cols // group, split, 0)
 
+    moment = time_ref[0].astype(F32)
+    half = d // 2
+    angles = tab_ref[2 * cols + 16 * height :, :] * moment
+    emb = jnp.concatenate([jnp.sin(angles), jnp.cos(angles)], axis=1)
+    temb = jnp.dot(
+        emb, w_time_ref[...].astype(F32),
+        precision=lax.Precision.HIGHEST, preferred_element_type=F32,
+    )[0:1]
+    w_in = w_in_ref[...].astype(F32)
+    w_in_s, w_in_p = w_in[:ch].astype(BF16), w_in[ch:].astype(BF16)
+
     pl.semaphore_wait(barrier, ndom - 1 + nrow - 1)
     sends = []
     for k in range(1, ndom):
@@ -154,18 +165,22 @@
         copy.start()
         sends.append(copy)
 
-    temb = jnp.dot(
-        emb_ref[...], w_time_ref[...].astype(F32),
-        precision=lax.Precision.HIGHEST, preferred_element_type=F32,
-    )[0:1]
-    w_in = w_in_ref[...].astype(F32)
-    w_in_s, w_in_p = w_in[:ch].astype(BF16), w_in[ch:].astype(BF16)
-
     for copy in loads[:4]:
         copy.wait()
     cos_r, sin_r = tab_ref[0:cols], tab_ref[cols : 2 * cols]
     step_rows = 2 if rows % 2 == 0 else 1
     n0 = step_rows * cols
+
+    def h_copy(i, k):
+        peer = lax.rem(row + k, nrow)
+        return pltpu.make_async_remote_copy(
+            src_ref=h1.at[pl.ds(i * step_rows, step_rows), pl.ds(pl.multiple_of(peer * mine, mine), mine), :],
+            dst_ref=hcol.at[pl.ds(row * rows + i * step_rows, step_rows)],
+            send_sem=h_send.at[i, k],
+            recv_sem=h_recv.at[i, k],
+            device_id={"row": peer},
+            device_id_type=MESH,
+        )
 
     def first(i, carry):
         sl = pl.ds(pl.multiple_of(i * n0, n0), n0)
@@ -188,43 +203,44 @@
         h = (h + mm(o, w_attn[0])).astype(BF16).astype(F32)
         h = mlp(h, w_up[0], w_down[0])
         h1[pl.ds(i * step_rows, step_rows)] = h.reshape(step_rows, cols, d)
+        for k in range(1, nrow):
+            h_copy(i, k).start()
         return carry
 
     lax.fori_loop(0, rows // step_rows, first, 0)
 
-    hs = []
-    for k in range(1, nrow):
-        peer = lax.rem(row + k, nrow)
-        copy = pltpu.make_async_remote_copy(
-            src_ref=h1.at[:, pl.ds(pl.multiple_of(peer * mine, mine), mine), :],
-            dst_ref=hcol.at[pl.ds(row * rows, rows)],
-            send_sem=h_send.at[k],
-            recv_sem=h_recv.at[k],
-            device_id={"row": peer},
-            device_id_type=MESH,
-        )
-        copy.start()
-        hs.append(copy)
     hcol[pl.ds(row * rows, rows)] = h1[:, pl.ds(pl.multiple_of(row * mine, mine), mine), :]
     for copy in loads[4:]:
         copy.wait()
-    for copy in hs:
-        copy.wait_recv()
 
     cos_c = tab_ref[2 * cols : 2 * cols + 8 * height].reshape(height, 8, LANES)
     sin_c = tab_ref[2 * cols + 8 * height : 2 * cols + 16 * height].reshape(height, 8, LANES)
-    wide = 16
     n1 = height * wide
     sub = height * 8
-    cos_c = jnp.concatenate([cos_c, cos_c], axis=1).reshape(n1, LANES)
-    sin_c = jnp.concatenate([sin_c, sin_c], axis=1).reshape(n1, LANES)
+    cos_c = jnp.concatenate([cos_c] * (wide // 8), axis=1).reshape(n1, LANES)
+    sin_c = jnp.concatenate([sin_c] * (wide // 8), axis=1).reshape(n1, LANES)
     per = LANES // head
     qi = lax.broadcasted_iota(jnp.int32, (sub, per * sub), 0)
     ki = lax.broadcasted_iota(jnp.int32, (sub, per * sub), 1)
     mask = jnp.where(qi % 8 == ki % 8, 1.0, 0.0).astype(F32)
-
-    def second(i, carry):
-        sl = pl.ds(pl.multiple_of(i * wide, wide), wide)
+    hlane = lax.broadcasted_iota(jnp.int32, (height, LANES), 1)
+
+    for i in range(rows // step_rows):
+        for k in range(1, nrow):
+            h_copy(i, k).wait_recv()
+
+    def g_copy(i, k):
+        return pltpu.make_async_remote_copy(
+            src_ref=gat[i].at[dom],
+            dst_ref=gat[i].at[dom],
+            send_sem=g_send.at[i, k],
+            recv_sem=g_recv.at[i, k],
+            device_id={"dom": lax.rem(dom + k, ndom)},
+            device_id_type=MESH,
+        )
+
+    def second(i):
+        sl = pl.ds(i * wide, wide)
         h = hcol[:, sl, :].reshape(n1, d).astype(F32)
         qkv = mm(rms(h).astype(BF16), w_qkv[1])
         q = rotated(qkv[:, :d], cos_c, sin_c, head)
@@ -246,79 +262,105 @@
         o = jnp.concatenate(mixed, axis=1).reshape(n1, d).astype(BF16)
         h = (h + mm(o, w_attn[1])).astype(BF16).astype(F32)
         h = mlp(h, w_up[1], w_down[1]).astype(F32)
-        pred = mm(rms(h).astype(BF16), w_out_ref[...])
-        psend[:, sl, 0:ch] = pred.astype(BF16).reshape(height, wide, ch)
-        return carry
-
-    lax.fori_loop(0, mine // wide, second, 0)
-
-    ps = []
-    for k in range(1, nrow):
-        peer = lax.rem(row + k, nrow)
-        copy = pltpu.make_async_remote_copy(
-            src_ref=psend.at[pl.ds(peer * rows, rows)],
-            dst_ref=ptok.at[:, pl.ds(pl.multiple_of(row * mine, mine), mine), :],
-            send_sem=p_send.at[k],
-            recv_sem=p_recv.at[k],
-            device_id={"row": peer},
-            device_id_type=MESH,
-        )
-        copy.start()
-        ps.append(copy)
-    ptok[:, pl.ds(pl.multiple_of(row * mine, mine), mine), :] = psend[pl.ds(row * rows, rows)]
-    for copy in ps:
-        copy.wait_recv()
-    for r in range(rows):
-        xs[r * cols : (r + 1) * cols, :] = ptok[r].astype(F32)
-
-    def join(c, carry):
-        base = c * glanes
-        toks = [xs[pl.ds(c * group + t, rows, stride=cols), :] for t in range(group)]
-        for j in range(glanes // LANES):
-            first_t, last_t = (j * LANES) // ch, (j * LANES + LANES - 1) // ch
+        ptok[:, 0:ch] = mm_nt(rms(h).astype(BF16), w_out_ref[...])
+        toks = [ptok[pl.ds(t, height, stride=wide), :] for t in range(wide)]
+        for j in range(flat // LANES):
+            first_t = (j * LANES) // ch
+            last_t = min((j * LANES + LANES - 1) // ch, wide - 1)
             acc = None
             for t in range(first_t, last_t + 1):
                 s = t * ch - j * LANES
-                v = pltpu.roll(toks[t], s % LANES, 1) if s % LANES else toks[t]
-                acc = v if acc is None else jnp.where(lane >= s, v, acc)
-            preds[dom, :, pl.ds(pl.multiple_of(base + j * LANES, LANES), LANES)] = acc.astype(BF16)
-        return carry
-
-    lax.fori_loop(0, cols // group, join, 0)
-
-    gs = []
-    for k in range(1, ndom):
-        copy = pltpu.make_async_remote_copy(
-            src_ref=preds.at[dom],
-            dst_ref=preds.at[dom],
-            send_sem=g_send.at[k],
-            recv_sem=g_recv.at[k],
-            device_id={"dom": lax.rem(dom + k, ndom)},
-            device_id_type=MESH,
-        )
-        copy.start()
-        gs.append(copy)
+                x = pltpu.roll(toks[t], s % LANES, 1) if s % LANES else toks[t]
+                acc = x if acc is None else jnp.where(hlane >= s, x, acc)
+            gat[i][dom, :, j * LANES : (j + 1) * LANES] = acc.astype(BF16)
+        for k in range(1, ndom):
+            g_copy(i, k).start()
+
+    for i in range(halves):
+        second(i)
+
     own.wait()
     for copy in sends:
         copy.wait()
-    for copy in gs:
-        copy.wait()
-    for copy in hs + ps:
-        copy.wait_send()
     a = anc_ref[dom]
-    c1, c2, c3 = coef_ref[0], coef_ref[1], coef_ref[2]
-    for c in range(cols // group):
-        sl = pl.ds(c * glanes, glanes)
-        p = preds[a, :, sl]
-        pw = p.astype(F32)
-        st = states[a, :, sl].astype(F32)
-        new_pred_ref[0, :, sl] = p
-        new_state_ref[0, :, sl] = (c2 * pw + c3 * (st - c1 * pw)).astype(BF16)
+    state_out[0] = states[a]
+
+    def p_copy(i, k):
+        peer = lax.rem(row + k, nrow)
+        return pltpu.make_async_remote_copy(
+            src_ref=sel.at[i, peer],
+            dst_ref=fin.at[row, i],
+            send_sem=p_send.at[i, k],
+            recv_sem=p_recv.at[i, k],
+            device_id={"row": peer},
+            device_id_type=MESH,
+        )
+
+    for i in range(halves):
+        for k in range(1, ndom):
+            g_copy(i, k).wait_recv()
+        selw[...] = gat[i][a].astype(F32)
+        for r in range(nrow):
+            sel[i, r] = selw[r * rows : (r + 1) * rows, :].astype(BF16)
+        for k in range(1, nrow):
+            p_copy(i, k).start()
+        fin[row, i] = sel[i, row]
+    for i in range(halves):
+        for k in range(1, nrow):
+            p_copy(i, k).wait_recv()
+
+    size = wide * ch
+    count = flat // LANES
+
+    def piece(q, offset):
+        r, i = divmod(q, halves)
+        tile, rem = divmod(offset, LANES)
+
+        def load(j):
+            x = fin[r, i, :, j * LANES : (j + 1) * LANES].astype(F32)
+            return pltpu.roll(x, LANES - rem, 1) if rem else x
+
+        low = load(tile) if tile >= 0 else None
+        if not rem or tile + 1 >= count:
+            return low
+        high = load(tile + 1)
+        return high if low is None else jnp.where(lane < LANES - rem, low, high)
+
+    for j in range(cols * ch // LANES):
+        start = j * LANES
+        acc = None
+        for q in range(start // size, (start + LANES - 1) // size + 1):
+            x = piece(q, start - q * size)
+            acc = x if acc is None else jnp.where(lane >= q * size - start, x, acc)
+        pred_out[0, :, start : start + LANES] = acc.astype(BF16)
+
+    for i in range(rows // step_rows):
+        for k in range(1, nrow):
+            h_copy(i, k).wait_send()
+    for i in range(halves):
+        for k in range(1, ndom):
+            g_copy(i, k).wait_send()
+        for k in range(1, nrow):
+            p_copy(i, k).wait_send()
 
 
 def level(moment):
     cosine = jnp.cos((moment / STEPS + 0.008) / 1.008 * math.pi / 2.0)
     return cosine * cosine
+
+
+def update(time_ref, state_ref, pred_ref, new_state_ref, new_pred_ref):
+    moment = jnp.broadcast_to(time_ref[0].astype(F32), (1, LANES))
+    now, nxt = level(moment), level(moment - STRIDE)
+    c1, c2 = jnp.sqrt(now), jnp.sqrt(nxt)
+    c3 = jnp.sqrt(1.0 - nxt) / jnp.sqrt(1.0 - now)
+    for j in range(pred_ref.shape[-1] // LANES):
+        sl = slice(j * LANES, (j + 1) * LANES)
+        p = pred_ref[0, :, sl]
+        wide = p.astype(F32)
+        st = state_ref[0, :, sl].astype(F32)
+        new_pred_ref[0, :, sl] = p
+        new_state_ref[0, :, sl] = (c2 * wide + c3 * (st - c1 * wide)).astype(BF16)
 
 
 def per_device(
@@ -329,29 +371,32 @@
     d, ch = w_out.shape
     cols, height, head = width // ch, rows * nrow, d // HEADS
     ff = w_up.shape[2]
-    moment = timestep[0].astype(F32)
-    half = w_time.shape[0] // 2
-    rates = jnp.exp(-math.log(10000.0) * jnp.arange(half, dtype=F32) / half)
-    emb = jnp.concatenate([jnp.sin(moment * rates), jnp.cos(moment * rates)])
-    emb = jnp.broadcast_to(emb[None], (8, 2 * half))
-    now, nxt = level(moment), level(moment - STRIDE)
-    coef = jnp.stack([jnp.sqrt(now), jnp.sqrt(nxt), jnp.sqrt(1.0 - nxt) / jnp.sqrt(1.0 - now)])
+    half = d // 2
+    rates = np.exp(-math.log(10000.0) * np.arange(half) / half).astype(np.float32)
     cos_r, sin_r = rope_tables(cols, head)
     cos_c, sin_c = rope_tables(height, head)
     tables = jnp.asarray(
-        np.concatenate([cos_r, sin_r, np.repeat(cos_c, 8, axis=0), np.repeat(sin_c, 8, axis=0)])
+        np.concatenate(
+            [
+                cos_r, sin_r, np.repeat(cos_c, 8, axis=0), np.repeat(sin_c, 8, axis=0),
+                np.tile(rates[None], (8, 1)),
+            ]
+        )
     )
-    cfg = (ndom, nrow, rows, cols, ch, d, head, height)
     mine = cols // nrow
+    wide = min(16, mine)
+    flat = -(-wide * ch // LANES) * LANES
+    halves, steps = mine // wide, max(rows // 2, 1)
+    cfg = (ndom, nrow, rows, cols, ch, d, head, height, wide, flat)
     smem = pl.BlockSpec(memory_space=pltpu.SMEM)
     vmem = pl.BlockSpec(memory_space=pltpu.VMEM)
     hbm = pl.BlockSpec(memory_space=pl.ANY)
-    flat = jax.ShapeDtypeStruct((1, rows, width), BF16)
+    whole = jax.ShapeDtypeStruct((1, rows, width), BF16)
     dma = pltpu.SemaphoreType.DMA
-    return pl.pallas_call(
+    chosen, predicted = pl.pallas_call(
         functools.partial(kernel, cfg),
-        out_shape=(flat, flat),
-        in_specs=[smem, smem, vmem, vmem, vmem, vmem, vmem, vmem, hbm, hbm, hbm, hbm, vmem],
+        out_shape=(whole, whole),
+        in_specs=[smem, smem, vmem, vmem, vmem, vmem, vmem, hbm, hbm, hbm, hbm, vmem],
         out_specs=(vmem, vmem),
         scratch_shapes=[
             pltpu.VMEM((2, d, 3 * d), BF16),
@@ -362,28 +407,37 @@
             pltpu.VMEM((rows * cols, LANES), F32),
             pltpu.VMEM((rows, cols, d), BF16),
             pltpu.VMEM((height, mine, d), BF16),
-            pltpu.VMEM((height, mine, LANES), BF16),
-            pltpu.VMEM((rows, cols, LANES), BF16),
-            pltpu.VMEM((ndom, rows, width), BF16),
+            pltpu.VMEM((height * wide, LANES), F32),
+            [pltpu.VMEM((ndom, height, flat), BF16)] * halves,
+            pltpu.VMEM((height, flat), F32),
+            pltpu.VMEM((halves, nrow, rows, flat), BF16),
+            pltpu.VMEM((nrow, halves, rows, flat), BF16),
             pltpu.VMEM((ndom, rows, width), BF16),
             dma((2, 4)),
             dma,
             dma((ndom,)),
             dma((ndom,)),
-            dma((nrow,)),
-            dma((nrow,)),
-            dma((nrow,)),
-            dma((nrow,)),
-            dma((ndom,)),
-            dma((ndom,)),
+            dma((steps, nrow)),
+            dma((steps, nrow)),
+            dma((halves, ndom)),
+            dma((halves, ndom)),
+            dma((halves, nrow)),
+            dma((halves, nrow)),
         ],
         compiler_params=pltpu.CompilerParams(
             collective_id=0, has_side_effects=True, vmem_limit_bytes=56 * 1024 * 1024
         ),
     )(
-        ancestors, coef, state, prev_pred, emb, tables, w_in, w_time,
-        w_qkv, w_attn_out, w_up, w_down, w_out,
+        ancestors, timestep, state, prev_pred, tables, w_in, w_time,
+        w_qkv, w_attn_out, w_up, w_down, w_out.T,
     )
+    return pl.pallas_call(
+        update,
+        out_shape=(whole, whole),
+        in_specs=[smem, vmem, vmem],
+        out_specs=(vmem, vmem),
+        compiler_params=pltpu.CompilerParams(vmem_limit_bytes=4 * 1024 * 1024),
+    )(timestep, chosen, predicted)
 
 
 def solution(mesh):

time: 39.8 us -> 34.4 us (0.86)
  Pallas kernels: 33.7 us -> 31.1 us
  local copies, waits for them, and re-layouts: 3.57 us -> 1.77 us
  other arithmetic: 0.71 us -> 0 us
    pallas_call x1 -> x2, Pallas kernels: 33.7 us -> 31.1 us  [the longest x1 30.3 us: per_device(): pl.pallas_call(functools.partial(kernel, cfg), out_shape=(whole, whole),...]
    unnamed x7 -> x4, local copies, waits for them, and re-layouts: 2.97 us -> 1.77 us
    another operation x1 -> x0, other arithmetic: 0.65 us -> none  [per_device(): jnp.stack([jnp.sqrt(now), jnp.sqrt(nxt), jnp.sqrt(1.0 - nxt) / jnp.sqrt(1...]
    broadcast_in_dim x1 -> x0, local copies, waits for them, and re-layouts: 0.6 us -> none  [per_device(): emb = jnp.broadcast_to(emb[None], (8, 2 * half))]
where the time goes in v2:
time: 34.4 us; the launch traced here: 34.1 us
  Pallas kernels  31.1 us (90%)
  local copies, waits for them, and re-layouts  1.77 us (5%)
  between operations  1.3 us (4%)
    pallas_call x1, Pallas kernels, per_device(): pl.pallas_call(functools.partial(kernel, cfg), out_shape=(whole, whole),...  30.3 us
    unnamed x4, local copies, waits for them, and re-layouts  1.77 us
    pallas_call x1, Pallas kernels, per_device(): pl.pallas_call(update, out_shape=(whole, whole), in_specs=[smem, vmem, vm...  0.82 us

profile of v2, /device:TPU:0, one launch (start us, length us, event | category | flops | bytes accessed | tf_op | source)
XLA Modules:
  0.0 34.1 jit_solution(18429548605220233458)
XLA Ops:
  1.3 30.3 %shard_map.131 = (bf16[1,4,10752]{2,1,0:T(4,128)(2,1)}, bf16[1,4,10752]{2,1,0:T(4,128)(2,1)}) custom-call(s32[4]{0:T(128)} %anc_ref.1, s32[1]{0:T(128)S(6)} %copy.14.time_ref, bf16[1,4,10752]{2,1,0:T(4,128)(2,1)} %state_ref.1, bf16[1,4,10752]{2,1,0:T(4,128)(2,1)} %prev_ref.1, f32[520,128]{1,0:T(8,128)} %constant.2.clone.tab_ref, bf16[168,256]{1,0:T(8,128)(2,1)} %w_in_ref.1, ...), custom_call_target="tpu_custom_call" | custom-call | tf_op jit(solution)/shard_map/pallas_call | solution.py:396
  31.6 0.0 copy-start
  31.6 0.9 %copy-done = bf16[1,4,10752]{2,1,0:T(4,128)(2,1)S(1)} copy-done((bf16[1,4,10752]{2,1,0:T(4,128)(2,1)S(1)}, bf16[1,4,10752]{2,1,0:T(4,128)(2,1)}, u32[]{:S(2)}) %copy-start) | copy-done | bytes 86040
  32.4 0.0 copy-start.1
  32.4 0.9 %copy-done.1 = bf16[1,4,10752]{2,1,0:T(4,128)(2,1)S(1)} copy-done((bf16[1,4,10752]{2,1,0:T(4,128)(2,1)S(1)}, bf16[1,4,10752]{2,1,0:T(4,128)(2,1)}, u32[]{:S(2)}) %copy-start.1) | copy-done | bytes 86040
  33.3 0.8 %shard_map.132 = (bf16[1,4,10752]{2,1,0:T(4,128)(2,1)}, bf16[1,4,10752]{2,1,0:T(4,128)(2,1)}) custom-call(s32[1]{0:T(128)S(6)} %copy.14.time_ref, bf16[1,4,10752]{2,1,0:T(4,128)(2,1)S(1)} %copy-done, bf16[1,4,10752]{2,1,0:T(4,128)(2,1)S(1)} %copy-done.1), custom_call_target="tpu_custom_call" | custom-call | tf_op jit(solution)/shard_map/pallas_call | solution.py:434
Async XLA Ops:
  31.6 0.9 %copy-start = (bf16[1,4,10752]{2,1,0:T(4,128)(2,1)S(1)}, bf16[1,4,10752]{2,1,0:T(4,128)(2,1)}, u32[]{:S(2)}) copy-start(bf16[1,4,10752]{2,1,0:T(4,128)(2,1)} %get-tuple-element.4.state_ref) | copy-start | bytes 258052
  32.4 0.9 %copy-start.1 = (bf16[1,4,10752]{2,1,0:T(4,128)(2,1)S(1)}, bf16[1,4,10752]{2,1,0:T(4,128)(2,1)}, u32[]{:S(2)}) copy-start(bf16[1,4,10752]{2,1,0:T(4,128)(2,1)} %get-tuple-element.5.pred_ref) | copy-start | bytes 258052

commit v3 on v2

--- a/solution.py
+++ b/solution.py
@@ -395,7 +395,7 @@
     dma = pltpu.SemaphoreType.DMA
     chosen, predicted = pl.pallas_call(
         functools.partial(kernel, cfg),
-        out_shape=(whole, whole),
+        out_shape=(pltpu.VMEM((1, rows, width), BF16),) * 2,
         in_specs=[smem, smem, vmem, vmem, vmem, vmem, vmem, hbm, hbm, hbm, hbm, vmem],
         out_specs=(vmem, vmem),
         scratch_shapes=[

time: 34.4 us -> 31.9 us (0.927)
  local copies, waits for them, and re-layouts: 1.77 us -> 0 us
  Pallas kernels: 31.1 us -> 30.4 us
    unnamed x4 -> x0, local copies, waits for them, and re-layouts: 1.77 us -> none
    pallas_call x1, Pallas kernels: 30.3 us -> 29.6 us  [per_device(): pl.pallas_call(functools.partial(kernel, cfg), out_shape=(pltpu.VMEM((1,...]
where the time goes in v3:
time: 31.9 us; the launch traced here: 31.7 us
  Pallas kernels  30.4 us (95%)
  between operations  1.29 us (4%)
    pallas_call x1, Pallas kernels, per_device(): pl.pallas_call(functools.partial(kernel, cfg), out_shape=(pltpu.VMEM((1,...  29.6 us
    pallas_call x1, Pallas kernels, per_device(): pl.pallas_call(update, out_shape=(whole, whole), in_specs=[smem, vmem, vm...  0.82 us

profile of v3, /device:TPU:0, one launch (start us, length us, event | category | flops | bytes accessed | tf_op | source)
XLA Modules:
  0.0 31.7 jit_solution(13716227349237021924)
XLA Ops:
  1.3 29.6 %shard_map.131 = (bf16[1,4,10752]{2,1,0:T(4,128)(2,1)S(1)}, bf16[1,4,10752]{2,1,0:T(4,128)(2,1)S(1)}) custom-call(s32[4]{0:T(128)} %anc_ref.1, s32[1]{0:T(128)S(6)} %copy.14.time_ref, bf16[1,4,10752]{2,1,0:T(4,128)(2,1)} %state_ref.1, bf16[1,4,10752]{2,1,0:T(4,128)(2,1)} %prev_ref.1, f32[520,128]{1,0:T(8,128)} %constant.2.clone.tab_ref, ...), custom_call_target="tpu_custom_call" | custom-call | tf_op jit(solution)/shard_map/pallas_call | solution.py:396
  30.9 0.8 %shard_map.132 = (bf16[1,4,10752]{2,1,0:T(4,128)(2,1)}, bf16[1,4,10752]{2,1,0:T(4,128)(2,1)}) custom-call(s32[1]{0:T(128)S(6)} %copy.14.time_ref, bf16[1,4,10752]{2,1,0:T(4,128)(2,1)S(1)} %get-tuple-element.4.state_ref, bf16[1,4,10752]{2,1,0:T(4,128)(2,1)S(1)} %get-tuple-element.5.pred_ref), custom_call_target="tpu_custom_call" | custom-call | tf_op jit(solution)/shard_map/pallas_call | solution.py:434

commit v4 on v3

--- a/solution.py
+++ b/solution.py
@@ -94,12 +94,14 @@
     xs, xp, h1, hcol, ptok, gat, selw, sel, fin, states,
     w_sem, own_sem, st_send, st_recv, h_send, h_recv, g_send, g_recv, p_send, p_recv,
 ):
-    ndom, nrow, rows, cols, ch, d, head, height, wide, flat = cfg
+    ndom, nrow, rows, cols, ch, d, head, height, wide, flat, pair = cfg
     dom, row = lax.axis_index("dom"), lax.axis_index("row")
     mine = cols // nrow
     group = LANES // math.gcd(ch, LANES)
     glanes = group * ch
     halves = mine // wide
+    teams = ndom // pair
+    team, seat = lax.div(dom, pair), lax.rem(dom, pair)
 
     loads = []
     pairs = ((w_qkv_hbm, w_qkv), (w_attn_hbm, w_attn), (w_up_hbm, w_up), (w_down_hbm, w_down))
@@ -114,10 +116,15 @@
         pl.semaphore_signal(
             barrier, inc=1, device_id={"dom": lax.rem(dom + k, ndom)}, device_id_type=MESH
         )
-    for k in range(1, nrow):
-        pl.semaphore_signal(
-            barrier, inc=1, device_id={"row": lax.rem(row + k, nrow)}, device_id_type=MESH
-        )
+    for e in range(teams):
+        there = lax.rem(team + e, teams) * pair + seat
+        for k in range(1, nrow):
+            pl.semaphore_signal(
+                barrier,
+                inc=1,
+                device_id={"dom": there, "row": lax.rem(row + k, nrow)},
+                device_id_type=MESH,
+            )
     own = pltpu.make_async_copy(state_ref.at[0], states.at[dom], own_sem)
     own.start()
 
@@ -151,7 +158,7 @@
     w_in = w_in_ref[...].astype(F32)
     w_in_s, w_in_p = w_in[:ch].astype(BF16), w_in[ch:].astype(BF16)
 
-    pl.semaphore_wait(barrier, ndom - 1 + nrow - 1)
+    pl.semaphore_wait(barrier, ndom - 1 + teams * (nrow - 1))
     sends = []
     for k in range(1, ndom):
         copy = pltpu.make_async_remote_copy(
@@ -231,11 +238,11 @@
 
     def g_copy(i, k):
         return pltpu.make_async_remote_copy(
-            src_ref=gat[i].at[dom],
-            dst_ref=gat[i].at[dom],
+            src_ref=gat[i].at[seat],
+            dst_ref=gat[i].at[seat],
             send_sem=g_send.at[i, k],
             recv_sem=g_recv.at[i, k],
-            device_id={"dom": lax.rem(dom + k, ndom)},
+            device_id={"dom": team * pair + lax.rem(seat + k, pair)},
             device_id_type=MESH,
         )
 
@@ -272,42 +279,50 @@
                 s = t * ch - j * LANES
                 x = pltpu.roll(toks[t], s % LANES, 1) if s % LANES else toks[t]
                 acc = x if acc is None else jnp.where(hlane >= s, x, acc)
-            gat[i][dom, :, j * LANES : (j + 1) * LANES] = acc.astype(BF16)
-        for k in range(1, ndom):
+            gat[i][seat, :, j * LANES : (j + 1) * LANES] = acc.astype(BF16)
+        for k in range(1, pair):
             g_copy(i, k).start()
 
     for i in range(halves):
         second(i)
+
+    def p_copy(i, e, k):
+        there, peer = lax.rem(team + e, teams), lax.rem(row + k, nrow)
+        return pltpu.make_async_remote_copy(
+            src_ref=sel.at[i, there, peer],
+            dst_ref=fin[i].at[team, row],
+            send_sem=p_send.at[i, e, k],
+            recv_sem=p_recv.at[i, e, k],
+            device_id={"dom": there * pair + seat, "row": peer},
+            device_id_type=MESH,
+        )
+
+    others = [(e, k) for e in range(teams) for k in range(nrow) if (e, k) != (0, 0)]
+    others.sort(key=lambda x: (x[0] == 0, x))
+    for i in range(halves):
+        for k in range(1, pair):
+            g_copy(i, k).wait_recv()
+        for e in [*range(1, teams), 0]:
+            there = lax.rem(team + e, teams)
+            want = anc_ref[there * pair + seat] - team * pair
+            selw[...] = gat[i][jnp.clip(want, 0, pair - 1)].astype(F32)
+            for r in range(nrow):
+                sel[i, there, r] = selw[r * rows : (r + 1) * rows, :].astype(BF16)
+            for k in range(nrow):
+                if (e, k) != (0, 0):
+                    p_copy(i, e, k).start()
+        fin[i][team, row] = sel[i, team, row]
 
     own.wait()
     for copy in sends:
         copy.wait()
     a = anc_ref[dom]
     state_out[0] = states[a]
-
-    def p_copy(i, k):
-        peer = lax.rem(row + k, nrow)
-        return pltpu.make_async_remote_copy(
-            src_ref=sel.at[i, peer],
-            dst_ref=fin.at[row, i],
-            send_sem=p_send.at[i, k],
-            recv_sem=p_recv.at[i, k],
-            device_id={"row": peer},
-            device_id_type=MESH,
-        )
+    home = lax.div(a, pair)
 
     for i in range(halves):
-        for k in range(1, ndom):
-            g_copy(i, k).wait_recv()
-        selw[...] = gat[i][a].astype(F32)
-        for r in range(nrow):
-            sel[i, r] = selw[r * rows : (r + 1) * rows, :].astype(BF16)
-        for k in range(1, nrow):
-            p_copy(i, k).start()
-        fin[row, i] = sel[i, row]
-    for i in range(halves):
-        for k in range(1, nrow):
-            p_copy(i, k).wait_recv()
+        for e, k in others:
+            p_copy(i, e, k).wait_recv()
 
     size = wide * ch
     count = flat // LANES
@@ -317,7 +332,7 @@
         tile, rem = divmod(offset, LANES)
 
         def load(j):
-            x = fin[r, i, :, j * LANES : (j + 1) * LANES].astype(F32)
+            x = fin[i][home, r, :, j * LANES : (j + 1) * LANES].astype(F32)
             return pltpu.roll(x, LANES - rem, 1) if rem else x
 
         low = load(tile) if tile >= 0 else None
@@ -338,10 +353,10 @@
         for k in range(1, nrow):
             h_copy(i, k).wait_send()
     for i in range(halves):
-        for k in range(1, ndom):
+        for k in range(1, pair):
             g_copy(i, k).wait_send()
-        for k in range(1, nrow):
-            p_copy(i, k).wait_send()
+        for e, k in others:
+            p_copy(i, e, k).wait_send()
 
 
 def level(moment):
@@ -387,7 +402,9 @@
     wide = min(16, mine)
     flat = -(-wide * ch // LANES) * LANES
     halves, steps = mine // wide, max(rows // 2, 1)
-    cfg = (ndom, nrow, rows, cols, ch, d, head, height, wide, flat)
+    pair = max(p for p in range(1, ndom + 1) if ndom % p == 0 and p * p <= ndom)
+    teams = ndom // pair
+    cfg = (ndom, nrow, rows, cols, ch, d, head, height, wide, flat, pair)
     smem = pl.BlockSpec(memory_space=pltpu.SMEM)
     vmem = pl.BlockSpec(memory_space=pltpu.VMEM)
     hbm = pl.BlockSpec(memory_space=pl.ANY)
@@ -408,10 +425,10 @@
             pltpu.VMEM((rows, cols, d), BF16),
             pltpu.VMEM((height, mine, d), BF16),
             pltpu.VMEM((height * wide, LANES), F32),
-            [pltpu.VMEM((ndom, height, flat), BF16)] * halves,
+            [pltpu.VMEM((pair, height, flat), BF16)] * halves,
             pltpu.VMEM((height, flat), F32),
-            pltpu.VMEM((halves, nrow, rows, flat), BF16),
-            pltpu.VMEM((nrow, halves, rows, flat), BF16),
+            pltpu.VMEM((halves, teams, nrow, rows, flat), BF16),
+            [pltpu.VMEM((teams, nrow, rows, flat), BF16)] * halves,
             pltpu.VMEM((ndom, rows, width), BF16),
             dma((2, 4)),
             dma,
@@ -419,10 +436,10 @@
             dma((ndom,)),
             dma((steps, nrow)),
             dma((steps, nrow)),
-            dma((halves, ndom)),
-            dma((halves, ndom)),
-            dma((halves, nrow)),
-            dma((halves, nrow)),
+            dma((halves, pair)),
+            dma((halves, pair)),
+            dma((halves, teams, nrow)),
+            dma((halves, teams, nrow)),
         ],
         compiler_params=pltpu.CompilerParams(
             collective_id=0, has_side_effects=True, vmem_limit_bytes=56 * 1024 * 1024

time: 31.9 us -> 30.5 us (0.956)
  Pallas kernels: 30.4 us -> 29 us
    pallas_call x1, Pallas kernels: 29.6 us -> 28.2 us  [per_device(): pl.pallas_call(functools.partial(kernel, cfg), out_shape=(pltpu.VMEM((1,...]
where the time goes in v4:
time: 30.5 us; the launch traced here: 30.3 us
  Pallas kernels  29 us (95%)
  between operations  1.29 us (4%)
    pallas_call x1, Pallas kernels, per_device(): pl.pallas_call(functools.partial(kernel, cfg), out_shape=(pltpu.VMEM((1,...  28.2 us
    pallas_call x1, Pallas kernels, per_device(): pl.pallas_call(update, out_shape=(whole, whole), in_specs=[smem, vmem, vm...  0.82 us

profile of v4, /device:TPU:0, one launch (start us, length us, event | category | flops | bytes accessed | tf_op | source)
XLA Modules:
  0.0 30.3 jit_solution(13618596843335852663)
XLA Ops:
  1.3 28.2 %shard_map.131 = (bf16[1,4,10752]{2,1,0:T(4,128)(2,1)S(1)}, bf16[1,4,10752]{2,1,0:T(4,128)(2,1)S(1)}) custom-call(s32[4]{0:T(128)} %anc_ref.1, s32[1]{0:T(128)S(6)} %copy.14.time_ref, bf16[1,4,10752]{2,1,0:T(4,128)(2,1)} %state_ref.1, bf16[1,4,10752]{2,1,0:T(4,128)(2,1)} %prev_ref.1, f32[520,128]{1,0:T(8,128)} %constant.2.clone.tab_ref, ...), custom_call_target="tpu_custom_call" | custom-call | tf_op jit(solution)/shard_map/pallas_call | solution.py:413
  29.5 0.8 %shard_map.132 = (bf16[1,4,10752]{2,1,0:T(4,128)(2,1)}, bf16[1,4,10752]{2,1,0:T(4,128)(2,1)}) custom-call(s32[1]{0:T(128)S(6)} %copy.14.time_ref, bf16[1,4,10752]{2,1,0:T(4,128)(2,1)S(1)} %get-tuple-element.4.state_ref, bf16[1,4,10752]{2,1,0:T(4,128)(2,1)S(1)} %get-tuple-element.5.pred_ref), custom_call_target="tpu_custom_call" | custom-call | tf_op jit(solution)/shard_map/pallas_call | solution.py:451

commit v5 on v4

--- a/solution.py
+++ b/solution.py
@@ -40,8 +40,8 @@
     return cos.astype(np.float32), sin.astype(np.float32)
 
 
-def rotated(v, cos, sin, head):
-    inv = lax.rsqrt(jnp.mean(v * v, axis=-1, keepdims=True) + 1e-06)
+def rotated(v, cos, sin, head, scale=1.0):
+    inv = lax.rsqrt(jnp.mean(v * v, axis=-1, keepdims=True) + 1e-06) * scale
     lane = lax.broadcasted_iota(jnp.int32, (1, LANES), 1)
     low = (lane % head) < head // 2
     parts = []
@@ -60,7 +60,6 @@
     n = q[0].shape[0]
     lane = lax.broadcasted_iota(jnp.int32, (1, LANES), 1)
     per = LANES // head
-    scale = math.log2(math.e) / math.sqrt(head)
     outs = []
     for part in range(len(q)):
         keys, vals = [], []
@@ -71,7 +70,7 @@
                 jnp.concatenate([v[part] * pick, jnp.broadcast_to(pick, (n, LANES))], axis=1)
             )
         scores = mm_nt(q[part], jnp.concatenate(keys, axis=0))
-        weights = jnp.exp2(scores * scale)
+        weights = jnp.exp2(scores)
         if mask is not None:
             weights = weights * mask
         both = mm(weights.astype(BF16), jnp.concatenate(vals, axis=0))
@@ -81,7 +80,10 @@
 
 def mlp(h, w_up, w_down):
     lifted = mm(rms(h).astype(BF16), w_up)
-    gated = jax.nn.gelu(lifted, approximate=True).astype(BF16)
+    root = math.sqrt(2.0 / math.pi)
+    inner = lifted * (root + (root * 0.044715) * (lifted * lifted))
+    half = 0.5 * lifted
+    gated = (half + half * jnp.tanh(inner)).astype(BF16)
     return (h + mm(gated, w_down)).astype(BF16)
 
 
@@ -100,6 +102,7 @@
     group = LANES // math.gcd(ch, LANES)
     glanes = group * ch
     halves = mine // wide
+    scale = math.log2(math.e) / math.sqrt(head)
     teams = ndom // pair
     team, seat = lax.div(dom, pair), lax.rem(dom, pair)
 
@@ -149,6 +152,10 @@
 
     moment = time_ref[0].astype(F32)
     half = d // 2
+    times = jnp.broadcast_to(moment, (1, LANES))
+    now, nxt = level(times), level(times - STRIDE)
+    c1, c2 = jnp.sqrt(now), jnp.sqrt(nxt)
+    c3 = jnp.sqrt(1.0 - nxt) / jnp.sqrt(1.0 - now)
     angles = tab_ref[2 * cols + 16 * height :, :] * moment
     emb = jnp.concatenate([jnp.sin(angles), jnp.cos(angles)], axis=1)
     temb = jnp.dot(
@@ -196,7 +203,7 @@
         qkv = mm(rms(h).astype(BF16), w_qkv[0])
         cos = jnp.concatenate([cos_r] * step_rows, axis=0)
         sin = jnp.concatenate([sin_r] * step_rows, axis=0)
-        q = [x.astype(BF16) for x in rotated(qkv[:, :d], cos, sin, head)]
+        q = [x.astype(BF16) for x in rotated(qkv[:, :d], cos, sin, head, scale)]
         k = [x.astype(BF16) for x in rotated(qkv[:, d : 2 * d], cos, sin, head)]
         v = qkv[:, 2 * d :].astype(BF16)
         v = [v[:, p * LANES : (p + 1) * LANES] for p in range(d // LANES)]
@@ -250,7 +257,7 @@
         sl = pl.ds(i * wide, wide)
         h = hcol[:, sl, :].reshape(n1, d).astype(F32)
         qkv = mm(rms(h).astype(BF16), w_qkv[1])
-        q = rotated(qkv[:, :d], cos_c, sin_c, head)
+        q = rotated(qkv[:, :d], cos_c, sin_c, head, scale)
         k = rotated(qkv[:, d : 2 * d], cos_c, sin_c, head)
         v = [qkv[:, 2 * d + p * LANES : 2 * d + (p + 1) * LANES] for p in range(d // LANES)]
         mixed = []
@@ -317,7 +324,6 @@
     for copy in sends:
         copy.wait()
     a = anc_ref[dom]
-    state_out[0] = states[a]
     home = lax.div(a, pair)
 
     for i in range(halves):
@@ -347,7 +353,11 @@
         for q in range(start // size, (start + LANES - 1) // size + 1):
             x = piece(q, start - q * size)
             acc = x if acc is None else jnp.where(lane >= q * size - start, x, acc)
-        pred_out[0, :, start : start + LANES] = acc.astype(BF16)
+        acc = acc.astype(BF16)
+        pred_out[0, :, start : start + LANES] = acc
+        pred = acc.astype(F32)
+        old = states[a, :, start : start + LANES].astype(F32)
+        state_out[0, :, start : start + LANES] = (c2 * pred + c3 * (old - c1 * pred)).astype(BF16)
 
     for i in range(rows // step_rows):
         for k in range(1, nrow):
@@ -364,18 +374,13 @@
     return cosine * cosine
 
 
-def update(time_ref, state_ref, pred_ref, new_state_ref, new_pred_ref):
-    moment = jnp.broadcast_to(time_ref[0].astype(F32), (1, LANES))
-    now, nxt = level(moment), level(moment - STRIDE)
-    c1, c2 = jnp.sqrt(now), jnp.sqrt(nxt)
-    c3 = jnp.sqrt(1.0 - nxt) / jnp.sqrt(1.0 - now)
-    for j in range(pred_ref.shape[-1] // LANES):
-        sl = slice(j * LANES, (j + 1) * LANES)
-        p = pred_ref[0, :, sl]
-        wide = p.astype(F32)
-        st = state_ref[0, :, sl].astype(F32)
-        new_pred_ref[0, :, sl] = p
-        new_state_ref[0, :, sl] = (c2 * wide + c3 * (st - c1 * wide)).astype(BF16)
+def hand_out(state_ref, pred_ref, new_state_ref, new_pred_ref, sems):
+    first = pltpu.make_async_copy(state_ref, new_state_ref, sems.at[0])
+    second = pltpu.make_async_copy(pred_ref, new_pred_ref, sems.at[1])
+    first.start()
+    second.start()
+    first.wait()
+    second.wait()
 
 
 def per_device(
@@ -410,7 +415,7 @@
     hbm = pl.BlockSpec(memory_space=pl.ANY)
     whole = jax.ShapeDtypeStruct((1, rows, width), BF16)
     dma = pltpu.SemaphoreType.DMA
-    chosen, predicted = pl.pallas_call(
+    stepped, predicted = pl.pallas_call(
         functools.partial(kernel, cfg),
         out_shape=(pltpu.VMEM((1, rows, width), BF16),) * 2,
         in_specs=[smem, smem, vmem, vmem, vmem, vmem, vmem, hbm, hbm, hbm, hbm, vmem],
@@ -449,12 +454,13 @@
         w_qkv, w_attn_out, w_up, w_down, w_out.T,
     )
     return pl.pallas_call(
-        update,
+        hand_out,
         out_shape=(whole, whole),
-        in_specs=[smem, vmem, vmem],
-        out_specs=(vmem, vmem),
+        in_specs=[vmem, vmem],
+        out_specs=(hbm, hbm),
+        scratch_shapes=[dma((2,))],
         compiler_params=pltpu.CompilerParams(vmem_limit_bytes=4 * 1024 * 1024),
-    )(timestep, chosen, predicted)
+    )(stepped, predicted)
 
 
 def solution(mesh):

time: 30.5 us -> 30.3 us (level)
  no operation moved by 1% of the time
where the time goes in v5:
time: 30.3 us; the launch traced here: 30.2 us
  Pallas kernels  28.9 us (95%)
  between operations  1.29 us (4%)
    pallas_call x1, Pallas kernels, per_device(): pl.pallas_call(functools.partial(kernel, cfg), out_shape=(pltpu.VMEM((1,...  28.2 us
    pallas_call x1, Pallas kernels, per_device(): pl.pallas_call(hand_out, out_shape=(whole, whole), in_specs=[vmem, vmem],...  0.68 us

profile of v5, /device:TPU:0, one launch (start us, length us, event | category | flops | bytes accessed | tf_op | source)
XLA Modules:
  0.0 30.2 jit_solution(10743021453720934588)
XLA Ops:
  1.3 28.2 %shard_map.131 = (bf16[1,4,10752]{2,1,0:T(4,128)(2,1)S(1)}, bf16[1,4,10752]{2,1,0:T(4,128)(2,1)S(1)}) custom-call(s32[4]{0:T(128)} %anc_ref.1, s32[1]{0:T(128)S(6)} %copy.14.time_ref, bf16[1,4,10752]{2,1,0:T(4,128)(2,1)} %state_ref.1, bf16[1,4,10752]{2,1,0:T(4,128)(2,1)} %prev_ref.1, f32[520,128]{1,0:T(8,128)} %constant.2.clone.tab_ref, ...), custom_call_target="tpu_custom_call" | custom-call | tf_op jit(solution)/shard_map/pallas_call | solution.py:418
  29.5 0.7 %shard_map.132 = (bf16[1,4,10752]{2,1,0:T(4,128)(2,1)}, bf16[1,4,10752]{2,1,0:T(4,128)(2,1)}) custom-call(bf16[1,4,10752]{2,1,0:T(4,128)(2,1)S(1)} %get-tuple-element.4.state_ref, bf16[1,4,10752]{2,1,0:T(4,128)(2,1)S(1)} %get-tuple-element.5.pred_ref), custom_call_target="tpu_custom_call" | custom-call | tf_op jit(solution)/shard_map/pallas_call | solution.py:456
